TPU v7x, 512 devices: a whole 4x4x16 slice. The times are simulated.
512 devices in a mesh: wide: 64 (over z, x), narrow: 8 (over y, core).
Axes of the slice: x: 4, y: 4, z: 16, core: 2. Of those that a mesh axis runs over, the one named last changes fastest.
Arguments:
- integrals: bfloat16 [16384, 65536], P('wide', 'narrow'), may hold values from -0.0625 to 0.0625
- amp_tiles: bfloat16 [8, 786432], P('narrow', 'wide'), may hold values from -6 to 6
- row_orbitals: int32 [16384, 2], P('wide'), may hold values from 0 to 511
- orb_irrep: int32 [512], replicated, may hold values from 0 to 3
- occ_pairs: int32 [96, 2], replicated, may hold values from 0 to 15
- occ_irrep: int32 [16], replicated, may hold values from 0 to 3
Outputs:
- residual: float32 [16384, 96], P(('wide', 'narrow'))
All inputs are finite; a program needn't handle non-finite values.
Results may differ from a plain program's by a relative error of at most 0.0003.
Values may be sent and summed in bfloat16 or wider, within the bound.
A program may use at most 64 MiB of HBM per device.

v0:
```python
import jax
import jax.numpy as jnp
from jax import lax
from jax.sharding import PartitionSpec as P


def lookup_irrep(orbitals, table):
    hits = orbitals[..., None] == jnp.arange(table.shape[0], dtype=jnp.int32)
    return jnp.sum(jnp.where(hits, table, 0), axis=-1)


def shards(integrals, amp_tiles, row_orbitals, orb_irrep, occ_pairs, occ_irrep):
    pair_count = occ_pairs.shape[0]
    column_count = integrals.shape[1]
    row_labels = lookup_irrep(row_orbitals, orb_irrep)
    pair_labels = lookup_irrep(occ_pairs, occ_irrep)
    row_sym = jnp.bitwise_xor(row_labels[:, 0], row_labels[:, 1])
    pair_sym = jnp.bitwise_xor(pair_labels[:, 0], pair_labels[:, 1])
    keep = row_sym[:, None] == pair_sym[None, :]
    gathered = lax.all_gather(amp_tiles, "wide", axis=1, tiled=True)
    amplitudes = gathered.reshape(column_count, pair_count)
    block = jnp.dot(integrals, amplitudes, preferred_element_type=jnp.float32)
    return lax.psum_scatter(
        jnp.where(keep, block, jnp.zeros_like(block)), "narrow", scatter_dimension=0, tiled=True
    )


def solution(mesh):
    in_specs = (P("wide", "narrow"), P("narrow", "wide"), P("wide", None), P(), P(), P())
    out_specs = P(("wide", "narrow"), None)
    return jax.shard_map(shards, mesh=mesh, in_specs=in_specs, out_specs=out_specs, check_vma=False)
```

profile of v0, /device:TPU:4, one launch (start us, length us, event | category | flops | bytes accessed | tf_op | source)
XLA Modules:
  0.0 240.3 jit_solution(9293615291129486285)
XLA Ops:
  6.5 0.0 all-gather.2.cloned.1.call-start
  6.5 0.7 all-gather.2.cloned.1.call-update
  7.3 0.0 reduce-scatter.2.cloned.1.call-start
  7.3 0.8 select_reduce_fusion.1
  8.1 1.0 select_reduce_fusion
  9.1 147.8 %all-gather.2.cloned.1.call-done = bf16[1,786432]{1,0:T(2,128)(2,1)} async-done(((bf16[1,12288]{1,0:T(2,128)(2,1)}), bf16[1,786432]{1,0:T(2,128)(2,1)}) %all-gather.2.cloned.1.call-update) | async-done | bytes 1572880 | tf_op jit(solution)/shard_map/all_gather | solution.py:20
  156.8 34.8 %reduce = bf16[786432]{0:T(1024)(128)(2,1)} reduce(bf16[1,786432]{1,0:T(2,128)(2,1)} %all-gather.2.cloned.1.call-done, bf16[]{:T(256)} %constant.5), dimensions={0}, to_apply=%all_gather.3.reduce_sub_computation | reduce | bytes 3145730 | tf_op jit(solution)/shard_map/all_gather | solution.py:20
  191.6 3.2 %reshape.15 = bf16[8192,96]{1,0:T(8,128)(2,1)S(1)} reshape(bf16[786432]{0:T(1024)(128)(2,1)} %reduce) | data formatting | bytes 3145728 | tf_op jit(solution)/shard_map/reshape | solution.py:21
  194.9 4.1 %convolution_select_fusion = f32[256,96]{1,0:T(8,128)} fusion(bf16[256,8192]{1,0:T(8,128)(2,1)} %param.6, bf16[8192,96]{1,0:T(8,128)(2,1)S(1)} %reshape.15, s32[96]{0:T(128)S(1)} %xor_bitcast_fusion, s32[256]{0:T(256)S(1)} %bitcast.5), kind=kOutput, calls=%fused_computation | convolution fusion | flops 402702336 | bytes 5866880 | tf_op jit(solution)/shard_map/dot_general | solution.py:22
  198.9 0.0 reduce-scatter.2.cloned.1.call-update
  198.9 34.5 %reduce-scatter.2.cloned.1.call-done = f32[32,96]{1,0:T(8,128)} async-done(((f32[256,96]{1,0:T(8,128)}), f32[32,96]{1,0:T(8,128)}) %reduce-scatter.2.cloned.1.call-update) | async-done | bytes 12304 | tf_op jit(solution)/shard_map/reduce_scatter | solution.py:23
  (2 shorter events, 0.0 us)
Async XLA Ops:
  6.5 150.3 %all-gather.2.cloned.1.call-start = ((), (), s32[]{:S(2)}) async-start(), calls=%async_computation.1 | async-start | bytes 3194880 | tf_op jit(solution)/shard_map/all_gather | solution.py:20
  7.3 226.2 %reduce-scatter.2.cloned.1.call-start = ((), (), s32[]{:S(2)}) async-start(), calls=%async_computation.2 | async-start | bytes 147456 | tf_op jit(solution)/shard_map/reduce_scatter | solution.py:23
Sparse Core Ops, SparseCore 0:
  10.3 146.4 all-gather.1
  199.1 34.3 reduce-scatter.1
where the time goes:
time: 241 us; the launch traced here: 240 us
  waiting for transfers between devices  183 us (76%)
  other arithmetic  36.5 us (15%)
  between operations  13.4 us (6%)
  matrix products  4.07 us (2%)
  local copies, waits for them, and re-layouts  3.24 us (1%)
    all_gather x1, waiting for transfers between devices, shards(): gathered = lax.all_gather(amp_tiles, 'wide', axis=1, tiled=True)  148 us
    all_gather x1, other arithmetic, shards(): gathered = lax.all_gather(amp_tiles, 'wide', axis=1, tiled=True)  34.8 us
    reduce_scatter x1, waiting for transfers between devices, shards(): lax.psum_scatter(jnp.where(keep, block, jnp.zeros_like(block)), 'narrow',...  34.5 us
  transfers between devices with their start and end apart: 2, of which 2 were waited for; matrix products, arithmetic and copies ran while one was open for 1% of the time, Pallas kernels for 0%

commit v1 on v0

--- a/solution.py
+++ b/solution.py
@@ -2,6 +2,13 @@
 import jax.numpy as jnp
 from jax import lax
 from jax.sharding import PartitionSpec as P
+
+
+def exchange_gather(x, axis, dim):
+    size = lax.axis_size(axis)
+    tiles = jnp.stack([x for _ in range(size)])
+    tiles = lax.all_to_all(tiles, axis, split_axis=0, concat_axis=0)
+    return jnp.concatenate(tiles, axis=dim)
 
 
 def lookup_irrep(orbitals, table):
@@ -17,7 +24,7 @@
     row_sym = jnp.bitwise_xor(row_labels[:, 0], row_labels[:, 1])
     pair_sym = jnp.bitwise_xor(pair_labels[:, 0], pair_labels[:, 1])
     keep = row_sym[:, None] == pair_sym[None, :]
-    gathered = lax.all_gather(amp_tiles, "wide", axis=1, tiled=True)
+    gathered = exchange_gather(amp_tiles, "wide", 1)
     amplitudes = gathered.reshape(column_count, pair_count)
     block = jnp.dot(integrals, amplitudes, preferred_element_type=jnp.float32)
     return lax.psum_scatter(

time: 241 us -> 189 us (0.78)
  the two profiles are of different devices: /device:TPU:4 before, /device:TPU:2 now
where the time goes in v1:
time: 189 us; the launch traced here: 188 us
  waiting for transfers between devices  107 us (57%)
  other arithmetic  23.4 us (12%)
  local copies, waits for them, and re-layouts  21 us (11%)
  starting transfers between devices  19 us (10%)
  between operations  13.5 us (7%)
  matrix products  4.07 us (2%)
    all_to_all x1, waiting for transfers between devices, exchange_gather(): tiles = lax.all_to_all(tiles, axis, split_axis=0, concat_axis=0)  77.1 us
    reduce_scatter x1, waiting for transfers between devices, shards(): lax.psum_scatter(jnp.where(keep, block, jnp.zeros_like(block)), 'narrow',...  29.8 us
    all_to_all x1, starting transfers between devices, exchange_gather(): tiles = lax.all_to_all(tiles, axis, split_axis=0, concat_axis=0)  18.9 us
    unnamed x10, local copies, waits for them, and re-layouts  14 us
    another operation x1, other arithmetic, exchange_gather(): tiles = jnp.stack([x for _ in range(size)])  11.4 us
    all_to_all x1, other arithmetic, exchange_gather(): tiles = lax.all_to_all(tiles, axis, split_axis=0, concat_axis=0)  10.7 us
    dot_general x1, matrix products, shards(): block = jnp.dot(integrals, amplitudes, preferred_element_type=jnp.float32)  4.07 us
  transfers between devices with their start and end apart: 2, of which 2 were waited for; matrix products, arithmetic and copies ran while one was open for 0% of the time, Pallas kernels for 0%

profile of v1, /device:TPU:2, one launch (start us, length us, event | category | flops | bytes accessed | tf_op | source)
XLA Modules:
  0.0 187.9 jit_solution(1524057648933296750)
XLA Ops:
  6.5 0.9 reduce
  7.5 3.0 %stack.2 = bf16[64,1,12288]{2,1,0:T(2,128)(2,1)S(1)} broadcast(bf16[12288]{0:T(1024)(128)(2,1)S(1)} %reduce), dimensions={2} | broadcast | bytes 1597440 | tf_op jit(solution)/shard_map/stack | solution.py:9
  10.5 0.5 broadcast.7
  11.0 11.4 %reduce.2 = bf16[64,12288]{1,0:T(8,128)(2,1)} reduce(bf16[64,1,12288]{2,1,0:T(2,128)(2,1)S(1)} %stack.2, bf16[]{:T(256)} %broadcast.7), dimensions={1}, to_apply=%stack.2.reduce_sub_computation | reduce | bytes 3145730 | tf_op jit(solution)/shard_map/stack | solution.py:9
  22.4 4.9 %reshape.17 = bf16[64,2,6144]{2,1,0:T(2,128)(2,1)} reshape(bf16[64,12288]{1,0:T(8,128)(2,1)} %reduce.2) | data formatting | bytes 3145728
  27.3 0.0 copy-start.2
  27.3 0.0 copy-start.3
  27.3 0.0 copy-start
  27.3 0.0 copy-start.1
  27.3 18.9 %all-to-all-start = ((bf16[64,2,6144]{2,1,0:T(2,128)(2,1)}), bf16[64,2,6144]{2,1,0:T(2,128)(2,1)}, u32[]{:S(2)}, u32[]{:S(2)}) async-start(bf16[64,2,6144]{2,1,0:T(2,128)(2,1)} %reshape.17), calls=%async_computation | async-start | bytes 3145728 | tf_op jit(solution)/shard_map/all_to_all | solution.py:10
  46.3 0.0 reduce-scatter.2.cloned.1.call-start
  46.3 0.0 copy-done.2
  46.3 0.0 copy-done.3
  46.3 0.1 select_reduce_fusion.1
  46.4 0.0 copy-done
  46.4 0.0 copy-done.1
  46.4 0.3 select_reduce_fusion
  46.7 77.1 %all-to-all-done = bf16[64,2,6144]{2,1,0:T(2,128)(2,1)} async-done(((bf16[64,2,6144]{2,1,0:T(2,128)(2,1)}), bf16[64,2,6144]{2,1,0:T(2,128)(2,1)}, u32[]{:S(2)}, u32[]{:S(2)}) %all-to-all-start) | async-done | bytes 1572896 | tf_op jit(solution)/shard_map/all_to_all | solution.py:10
  123.8 9.1 %reshape.18 = bf16[64,1,12288]{2,1,0:T(2,128)(2,1)S(1)} reshape(bf16[64,2,6144]{2,1,0:T(2,128)(2,1)} %all-to-all-done) | data formatting | bytes 3145728
  132.9 10.7 %reduce.1 = bf16[64,12288]{1,0:T(8,128)(2,1)} reduce(bf16[64,1,12288]{2,1,0:T(2,128)(2,1)S(1)} %reshape.18, bf16[]{:T(256)} %constant.5), dimensions={1}, to_apply=%all_to_all.3.reduce_sub_computation | reduce | bytes 3145730 | tf_op jit(solution)/shard_map/all_to_all | solution.py:10
  143.7 3.4 %reshape_reshape.3 = bf16[8192,96]{1,0:T(8,128)(2,1)S(1)} reshape(bf16[64,12288]{1,0:T(8,128)(2,1)} %reduce.1) | data formatting | bytes 3145728 | tf_op jit(solution)/shard_map/reshape;reshape | solution.py:28
  147.1 4.1 %convolution_select_fusion = f32[256,96]{1,0:T(8,128)} fusion(bf16[256,8192]{1,0:T(8,128)(2,1)} %param.6, bf16[8192,96]{1,0:T(8,128)(2,1)S(1)} %reshape_reshape.3, s32[96]{0:T(128)S(1)} %xor_bitcast_fusion, s32[256]{0:T(256)S(1)} %bitcast.5), kind=kOutput, calls=%fused_computation | convolution fusion | flops 402702336 | bytes 5866880 | tf_op jit(solution)/shard_map/dot_general | solution.py:29
  151.2 0.0 reduce-scatter.2.cloned.1.call-update
  151.2 29.8 %reduce-scatter.2.cloned.1.call-done = f32[32,96]{1,0:T(8,128)} async-done(((f32[256,96]{1,0:T(8,128)}), f32[32,96]{1,0:T(8,128)}) %reduce-scatter.2.cloned.1.call-update) | async-done | bytes 12304 | tf_op jit(solution)/shard_map/reduce_scatter | solution.py:30
  (2 shorter events, 0.0 us)
Async XLA Ops:
  27.3 19.0 %copy-start.2 = (s32[96,2]{0,1:T(2,128)S(1)}, s32[96,2]{0,1:T(2,128)}, u32[]{:S(2)}) copy-start(s32[96,2]{0,1:T(2,128)} %param.10) | copy-start | bytes 2308
  27.3 19.0 %copy-start.3 = (s32[16]{0:T(128)S(1)}, s32[16]{0:T(128)}, u32[]{:S(2)}) copy-start(s32[16]{0:T(128)} %param.11) | copy-start | bytes 196
  27.3 19.1 %copy-start = (s32[512]{0:T(512)S(1)}, s32[512]{0:T(512)}, u32[]{:S(2)}) copy-start(s32[512]{0:T(512)} %param.9) | copy-start | bytes 6148
  27.3 19.1 %copy-start.1 = (s32[256,2]{0,1:T(2,128)S(1)}, s32[256,2]{0,1:T(2,128)}, u32[]{:S(2)}) copy-start(s32[256,2]{0,1:T(2,128)} %param.8) | copy-start | bytes 6148
  27.3 96.5 %all-to-all-start = ((bf16[64,2,6144]{2,1,0:T(2,128)(2,1)}), bf16[64,2,6144]{2,1,0:T(2,128)(2,1)}, u32[]{:S(2)}, u32[]{:S(2)}) async-start(bf16[64,2,6144]{2,1,0:T(2,128)(2,1)} %reshape.17), calls=%async_computation | async-start | bytes 3145728 | tf_op jit(solution)/shard_map/all_to_all | solution.py:10
  46.3 134.8 %reduce-scatter.2.cloned.1.call-start = ((), (), s32[]{:S(2)}) async-start(), calls=%async_computation.2 | async-start | bytes 147456 | tf_op jit(solution)/shard_map/reduce_scatter | solution.py:30
Sparse Core Ops, SparseCore 0:
  151.3 29.6 reduce-scatter.1
